TPU v7x, 32 devices: a whole 2x2x4 slice. The times are simulated.
32 devices in a mesh: row: 4 (over z), col: 4 (over y, x), depth: 2 (over core).
Axes of the slice: x: 2, y: 2, z: 4, core: 2. Of those that a mesh axis runs over, the one named last changes fastest.
Arguments:
- tiles: float32 [4, 4, 96, 256, 256], P('row', 'col', 'depth'), as said below
- tile_rows: int32 [4, 4, 96], P('row', 'col', 'depth'), may hold values from 0 to 127, as said below
- tile_cols: int32 [4, 4, 96], P('row', 'col', 'depth'), may hold values from 0 to 127
- tile_count: int32 [4, 4, 2], P('row', 'col', 'depth'), may hold values from 16 to 48, as said below
Outputs:
- row_scale: float32 [131072], P('row')
- col_scale: float32 [131072], P('col')
- scaled_tiles: float32 [4, 4, 96, 256, 256], P('row', 'col', 'depth')
Inputs may be any that keep to these rules, and one draw needn't show every extreme that they name: `tile_rows`: every block row and every block column of the matrix holds a live tile; no block is listed twice among the live tiles of the two depth lists of one row and col index. `tile_count`: some device's list is full in every draw. `tiles`: entries in empty slots are ignored.
All inputs are finite; a program needn't handle non-finite values.
Results may differ from a plain program's by a relative error of at most 0.0001.
Values sent between devices are 32-bit elements; how exact they have to be, the bound alone decides.
A program may use at most 128 MiB of HBM per device.

v0:
```python
import functools

import jax
import jax.numpy as jnp
from jax import lax
from jax.experimental import pallas as pl
from jax.experimental.pallas import tpu as pltpu
from jax.sharding import PartitionSpec as P

RB_DEV = 128
ANCHORS = 16
SWEEPS = 4
EPS = 1e-06
UNROLL = 8
MESH = pl.DeviceIdType.MESH
ROUNDS = SWEEPS + 1


def scale_kernel(
    rows, cols, count, tiles, r_out, c_out,
    mag, mag_t, load_sem, r_fac, c_fac, row_part, col_part,
    row_acc, col_acc, row_half, col_half, row_comb, col_comb, row_got, col_got,
    row_s1, row_r1, col_s1, col_r1, row_s2, row_r2, col_s2, col_r2, row_sg, row_rg, col_sg, col_rg,
):
    depths = lax.axis_size("depth")
    me_d = lax.axis_index("depth")
    slots, size = tiles.shape[0], tiles.shape[1]
    lanes = 128
    live = count[0]

    def load(s):
        return pltpu.make_async_copy(tiles.at[s], mag.at[s], load_sem.at[s])

    @pl.loop(0, slots)
    def _(s):
        load(s).start()

    def peers(axis):
        n = lax.axis_size(axis)
        me = lax.axis_index(axis)
        return [(k, {axis: lax.rem(me + k, n)}) for k in range(1, n)]

    barrier = pltpu.get_barrier_semaphore()
    greeted = 0
    for axis in ("row", "col", "depth"):
        for _, dev in peers(axis):
            pl.semaphore_signal(barrier, inc=1, device_id=dev, device_id_type=MESH)
            greeted += 1
    pl.semaphore_wait(barrier, greeted)

    class Side:
        def __init__(self, axis, fac, acc, half, comb, got, s1, r1, s2, r2, sg, rg):
            self.axis, self.fac, self.acc, self.half, self.comb, self.got = axis, fac, acc, half, comb, got
            self.s1, self.r1, self.s2, self.r2, self.sg, self.rg = s1, r1, s2, r2, sg, rg
            self.hb = acc.shape[2]

        def pair_copies(self, t):
            return [
                pltpu.make_async_remote_copy(
                    src_ref=self.acc.at[t, dev["depth"]], dst_ref=self.half.at[t, k - 1],
                    send_sem=self.s1.at[t, k - 1], recv_sem=self.r1.at[t, k - 1],
                    device_id=dev, device_id_type=MESH)
                for k, dev in peers("depth")
            ]

        def group_copies(self, t):
            return [
                pltpu.make_async_remote_copy(
                    src_ref=self.comb.at[t], dst_ref=self.got.at[t, k - 1],
                    send_sem=self.sg.at[t, k - 1], recv_sem=self.rg.at[t, k - 1],
                    device_id=dev, device_id_type=MESH)
                for k, dev in peers(self.axis)
            ]

        def back_copies(self, t):
            return [
                pltpu.make_async_remote_copy(
                    src_ref=self.fac.at[t + 1, me_d], dst_ref=self.fac.at[t + 1, me_d],
                    send_sem=self.s2.at[t, k - 1], recv_sem=self.r2.at[t, k - 1],
                    device_id=dev, device_id_type=MESH)
                for k, dev in peers("depth")
            ]

        def start_pair(self, t):
            for c in self.pair_copies(t):
                c.start()

        def pair_to_group(self, t, op):
            for c in self.pair_copies(t):
                c.wait()
            value = self.acc[t, me_d]
            for k in range(self.half.shape[1]):
                value = op(value, self.half[t, k])
            self.comb[t] = value
            for c in self.group_copies(t):
                c.start()

        def group_to_back(self, t, op):
            for c in self.group_copies(t):
                c.wait()
            value = self.comb[t]
            for k in range(self.got.shape[1]):
                value = op(value, self.got[t, k])
            now = self.fac[t, me_d]
            self.fac[t + 1, me_d] = now * lax.rsqrt(now * value + EPS)
            for c in self.back_copies(t):
                c.start()

        def finish_back(self, t):
            for c in self.back_copies(t):
                c.wait()

    row = Side("col", r_fac, row_acc, row_half, row_comb, row_got, row_s1, row_r1, row_s2, row_r2, row_sg, row_rg)
    col = Side("row", c_fac, col_acc, col_half, col_comb, col_got, col_s1, col_r1, col_s2, col_r2, col_sg, col_rg)

    def spread(side, t, part, ids, summed):
        shape = side.acc.shape[2:]
        for d in range(depths):
            block = lax.broadcasted_iota(jnp.int32, shape, 0) + d * side.hb

            def add(s, acc):
                term = jnp.where(block == ids[s], part[s], jnp.float32(0.0))
                return acc + term if summed else jnp.maximum(acc, term)

            side.acc[t, d] = lax.fori_loop(0, slots, add, jnp.zeros(shape, jnp.float32), unroll=4)

    def factor(side, t, index):
        return side.fac[t, index // side.hb, pl.ds(index % side.hb, 1), :]

    def down(f):
        return jnp.broadcast_to(f, (lanes, size)).T

    def fold(x, summed):
        return x.sum(axis=0, keepdims=True) if summed else x.max(axis=0, keepdims=True)

    def half_pass(other, side, values, part, here, there, t, summed):
        @pl.loop(0, slots, unroll=UNROLL)
        def _(s):
            f = down(factor(other, t, there[s]))
            for j in range(0, size, lanes):
                part[s, :, j:j + lanes] = fold(values[s, :, j:j + lanes] * f, summed)

        spread(side, t, part, here, summed)
        side.start_pair(t)

    def col_pass(t, summed):
        half_pass(row, col, mag, col_part, cols, rows, t, summed)

    def row_pass(t, summed):
        half_pass(col, row, mag_t, row_part, rows, cols, t, summed)

    r_fac[0] = jnp.ones(r_fac.shape[1:], jnp.float32)
    c_fac[0] = jnp.ones(c_fac.shape[1:], jnp.float32)

    @pl.loop(0, slots, unroll=2)
    def _(s):
        load(s).wait()
        u = jnp.where(s < live, jnp.abs(mag[s]), jnp.float32(0.0))
        mag[s] = u
        col_part[s] = fold(u, False)
        ut = u.T
        mag_t[s] = ut
        row_part[s] = fold(ut, False)

    spread(col, 0, col_part, cols, False)
    col.start_pair(0)
    spread(row, 0, row_part, rows, False)
    row.start_pair(0)
    col.pair_to_group(0, jnp.maximum)
    row.pair_to_group(0, jnp.maximum)

    def step(t, op, next_summed, last):
        next_op = jnp.add if next_summed else jnp.maximum
        row.group_to_back(t, op)
        row.finish_back(t)
        if not last:
            col_pass(t + 1, next_summed)
        col.group_to_back(t, op)
        if not last:
            col.pair_to_group(t + 1, next_op)
        col.finish_back(t)
        if not last:
            row_pass(t + 1, next_summed)
            row.pair_to_group(t + 1, next_op)

    @pl.loop(0, SWEEPS - 1)
    def _(t):
        step(t, jnp.maximum, False, False)

    step(SWEEPS - 1, jnp.maximum, True, False)
    step(SWEEPS, jnp.add, False, True)
    r_out[...] = r_fac[ROUNDS]
    c_out[...] = c_fac[ROUNDS]


def final_kernel(rows, cols, count, tiles, r_fac, c_fac, out):
    group, size = tiles.shape[0], tiles.shape[1]
    lanes = 128
    base = pl.program_id(0) * group

    @pl.when(base < count[0])
    def _():
        for k in range(group):
            s = base + k
            r = jnp.where(s < count[0], r_fac[pl.ds(rows[s], 1), :], jnp.float32(0.0))
            c = c_fac[pl.ds(cols[s], 1), :]
            rt = jnp.broadcast_to(r, (lanes, size)).T
            for j in range(0, size, lanes):
                out[k, :, j:j + lanes] = tiles[k, :, j:j + lanes] * rt * c[:, j:j + lanes]

    @pl.when(base >= count[0])
    def _():
        out[...] = jnp.zeros_like(out)


def shards(tiles, tile_rows, tile_cols, tile_count):
    values = tiles[0, 0]
    rows = tile_rows.reshape(-1)
    cols = tile_cols.reshape(-1)
    count = tile_count.reshape(-1)
    slots, size = values.shape[0], values.shape[1]
    n_row, n_col, depths = lax.axis_size("row"), lax.axis_size("col"), lax.axis_size("depth")
    col_blocks = n_row * depths * ANCHORS
    rh, ch = RB_DEV // depths, col_blocks // depths
    f32 = jnp.float32
    dma = pltpu.SemaphoreType.DMA
    d1 = depths - 1
    smem = pl.BlockSpec(memory_space=pltpu.SMEM)
    vmem = pl.BlockSpec(memory_space=pltpu.VMEM)
    row_scale, col_scale = pl.pallas_call(
        scale_kernel,
        out_shape=(
            jax.ShapeDtypeStruct((depths, rh, size), f32),
            jax.ShapeDtypeStruct((depths, ch, size), f32),
        ),
        in_specs=[smem, smem, smem, pl.BlockSpec(memory_space=pl.ANY)],
        out_specs=(vmem, vmem),
        scratch_shapes=[
            pltpu.VMEM((slots, size, size), f32),
            pltpu.VMEM((slots, size, size), f32),
            dma((slots,)),
            pltpu.VMEM((ROUNDS + 1, depths, rh, size), f32),
            pltpu.VMEM((ROUNDS + 1, depths, ch, size), f32),
            pltpu.VMEM((slots, 1, size), f32),
            pltpu.VMEM((slots, 1, size), f32),
            pltpu.VMEM((ROUNDS, depths, rh, size), f32),
            pltpu.VMEM((ROUNDS, depths, ch, size), f32),
            pltpu.VMEM((ROUNDS, d1, rh, size), f32),
            pltpu.VMEM((ROUNDS, d1, ch, size), f32),
            pltpu.VMEM((ROUNDS, rh, size), f32),
            pltpu.VMEM((ROUNDS, ch, size), f32),
            pltpu.VMEM((ROUNDS, n_col - 1, rh, size), f32),
            pltpu.VMEM((ROUNDS, n_row - 1, ch, size), f32),
            dma((ROUNDS, d1)), dma((ROUNDS, d1)), dma((ROUNDS, d1)), dma((ROUNDS, d1)),
            dma((ROUNDS, d1)), dma((ROUNDS, d1)), dma((ROUNDS, d1)), dma((ROUNDS, d1)),
            dma((ROUNDS, n_col - 1)), dma((ROUNDS, n_col - 1)),
            dma((ROUNDS, n_row - 1)), dma((ROUNDS, n_row - 1)),
        ],
        compiler_params=pltpu.CompilerParams(
            collective_id=0, has_side_effects=True, vmem_limit_bytes=60 * 2**20
        ),
        name="equilibrate",
    )(rows, cols, count, values)
    row_scale = row_scale.reshape(depths * rh, size)
    col_scale = col_scale.reshape(depths * ch, size)

    group = next(g for g in (4, 3, 2, 1) if slots % g == 0)
    whole = lambda shape: pl.BlockSpec(shape, lambda g, *_: (0, 0))

    def in_map(g, rows, cols, count):
        return (jnp.minimum(g, jnp.maximum(count[0] - 1, 0) // group), 0, 0)

    scaled = pl.pallas_call(
        final_kernel,
        grid_spec=pltpu.PrefetchScalarGridSpec(
            num_scalar_prefetch=3,
            grid=(slots // group,),
            in_specs=[
                pl.BlockSpec((group, size, size), in_map),
                whole(row_scale.shape),
                whole(col_scale.shape),
            ],
            out_specs=pl.BlockSpec((group, size, size), lambda g, *_: (g, 0, 0)),
        ),
        out_shape=jax.ShapeDtypeStruct(values.shape, f32),
        name="scale_tiles",
    )(rows, cols, count, values, row_scale, col_scale)
    return (row_scale.reshape(-1), col_scale.reshape(-1), scaled[None, None])


def solution(mesh):
    in_specs = (
        P("row", "col", "depth", None, None),
        P("row", "col", "depth"),
        P("row", "col", "depth"),
        P("row", "col", "depth"),
    )
    out_specs = (P("row"), P("col"), P("row", "col", "depth", None, None))
    return jax.shard_map(shards, mesh=mesh, in_specs=in_specs, out_specs=out_specs, check_vma=False)
```

profile of v0, /device:TPU:0, one launch (start us, length us, event | category | flops | bytes accessed | tf_op | source)
XLA Modules:
  0.0 96.2 jit_solution(13906602689243666609)
XLA Ops:
  1.3 81.1 %equilibrate.1 = (f32[2,64,256]{2,1,0:T(8,128)}, f32[2,64,256]{2,1,0:T(8,128)}) custom-call(s32[48]{0:T(128)} %bitcast.22, s32[48]{0:T(128)} %bitcast.24, s32[1]{0:T(128)} %bitcast.11.count, f32[48,256,256]{2,1,0:T(8,128)} %bitcast.13), custom_call_target="tpu_custom_call" | custom-call | tf_op jit(solution)/shard_map/equilibrate/pallas_call | solution.py:230
  82.4 0.0 copy-start.1
  82.4 0.0 copy-start
  82.4 12.4 %scale_tiles.1 = f32[48,256,256]{2,1,0:T(8,128)} custom-call(s32[48]{0:T(128)} %bitcast.23, s32[48]{0:T(128)} %bitcast.25, s32[1]{0:T(128)} %bitcast.12.count, f32[48,256,256]{2,1,0:T(8,128)} %bitcast.14, f32[128,256]{1,0:T(8,128)} %bitcast.16, f32[128,256]{1,0:T(8,128)} %bitcast.18), custom_call_target="tpu_custom_call" | custom-call | tf_op jit(solution)/shard_map/scale_tiles/pallas_call | solution.py:273
  94.8 0.0 copy-done.1
  94.8 0.7 copy.8
  95.5 0.0 copy-done
  95.5 0.7 copy.7
Async XLA Ops:
  82.4 12.4 %copy-start.1 = (f32[2,64,256]{2,1,0:T(8,128)S(1)}, f32[2,64,256]{2,1,0:T(8,128)}, u32[]{:S(2)}) copy-start(f32[2,64,256]{2,1,0:T(8,128)} %get-tuple-element.6) | copy-start | bytes 393220
  82.4 13.2 %copy-start = (f32[2,64,256]{2,1,0:T(8,128)S(1)}, f32[2,64,256]{2,1,0:T(8,128)}, u32[]{:S(2)}) copy-start(f32[2,64,256]{2,1,0:T(8,128)} %get-tuple-element.5) | copy-start | bytes 393220
where the time goes:
time: 97.6 us; the launch traced here: 96.2 us
  Pallas kernels  93.5 us (96%)
  local copies, waits for them, and re-layouts  1.45 us (1%)
  between operations  1.3 us (1%)
    pallas_call x1, Pallas kernels, shards(): pl.pallas_call(scale_kernel, out_shape=(jax.ShapeDtypeStruct((depths, rh,...  81.1 us
    pallas_call x1, Pallas kernels, shards(): pl.pallas_call(final_kernel, grid_spec=pltpu.PrefetchScalarGridSpec(num_s...  12.4 us

commit v1 on v0

--- a/solution.py
+++ b/solution.py
@@ -12,6 +12,7 @@
 SWEEPS = 4
 EPS = 1e-06
 UNROLL = 8
+GROUP = 4
 MESH = pl.DeviceIdType.MESH
 ROUNDS = SWEEPS + 1
 
@@ -158,9 +159,8 @@
         u = jnp.where(s < live, jnp.abs(mag[s]), jnp.float32(0.0))
         mag[s] = u
         col_part[s] = fold(u, False)
-        ut = u.T
-        mag_t[s] = ut
-        row_part[s] = fold(ut, False)
+        wide = functools.reduce(jnp.maximum, [u[:, j:j + lanes] for j in range(0, size, lanes)])
+        row_part[s] = fold(wide.T, False)
 
     spread(col, 0, col_part, cols, False)
     col.start_pair(0)
@@ -168,6 +168,10 @@
     row.start_pair(0)
     col.pair_to_group(0, jnp.maximum)
     row.pair_to_group(0, jnp.maximum)
+
+    @pl.loop(0, slots, unroll=4)
+    def _(s):
+        mag_t[s] = mag[s].T
 
     def step(t, op, next_summed, last):
         next_op = jnp.add if next_summed else jnp.maximum
@@ -193,24 +197,56 @@
     c_out[...] = c_fac[ROUNDS]
 
 
-def final_kernel(rows, cols, count, tiles, r_fac, c_fac, out):
-    group, size = tiles.shape[0], tiles.shape[1]
+def final_kernel(rows, cols, count, tiles, r_fac, c_fac, out, held, made, zero, in_sem, out_sem):
+    slots, size = tiles.shape[0], tiles.shape[1]
+    group = GROUP if slots % GROUP == 0 else 1
     lanes = 128
-    base = pl.program_id(0) * group
-
-    @pl.when(base < count[0])
-    def _():
-        for k in range(group):
-            s = base + k
-            r = jnp.where(s < count[0], r_fac[pl.ds(rows[s], 1), :], jnp.float32(0.0))
-            c = c_fac[pl.ds(cols[s], 1), :]
-            rt = jnp.broadcast_to(r, (lanes, size)).T
-            for j in range(0, size, lanes):
-                out[k, :, j:j + lanes] = tiles[k, :, j:j + lanes] * rt * c[:, j:j + lanes]
-
-    @pl.when(base >= count[0])
-    def _():
-        out[...] = jnp.zeros_like(out)
+    live = count[0]
+
+    def load(s):
+        return pltpu.make_async_copy(tiles.at[s], held.at[s], in_sem.at[s])
+
+    def store(s):
+        return pltpu.make_async_copy(made.at[s], out.at[s], out_sem.at[s])
+
+    @pl.loop(0, slots)
+    def _(s):
+        @pl.when(s // group * group < live)
+        def _():
+            load(s).start()
+
+    zero[...] = jnp.zeros_like(zero)
+
+    @pl.loop(0, slots // group)
+    def _(g):
+        base = g * group
+
+        @pl.when(base >= live)
+        def _():
+            for k in range(group):
+                pltpu.make_async_copy(zero, out.at[base + k], out_sem.at[base + k]).start()
+
+    @pl.loop(0, slots // group)
+    def _(g):
+        base = g * group
+
+        @pl.when(base < live)
+        def _():
+            for k in range(group):
+                load(base + k).wait()
+            for k in range(group):
+                s = base + k
+                r = jnp.where(s < live, r_fac[pl.ds(rows[s], 1), :], jnp.float32(0.0))
+                c = c_fac[pl.ds(cols[s], 1), :]
+                rt = jnp.broadcast_to(r, (lanes, size)).T
+                for j in range(0, size, lanes):
+                    made[s, :, j:j + lanes] = held[s, :, j:j + lanes] * rt * c[:, j:j + lanes]
+            for k in range(group):
+                store(base + k).start()
+
+    @pl.loop(0, slots)
+    def _(s):
+        store(s).wait()
 
 
 def shards(tiles, tile_rows, tile_cols, tile_count):
@@ -264,25 +300,19 @@
     row_scale = row_scale.reshape(depths * rh, size)
     col_scale = col_scale.reshape(depths * ch, size)
 
-    group = next(g for g in (4, 3, 2, 1) if slots % g == 0)
-    whole = lambda shape: pl.BlockSpec(shape, lambda g, *_: (0, 0))
-
-    def in_map(g, rows, cols, count):
-        return (jnp.minimum(g, jnp.maximum(count[0] - 1, 0) // group), 0, 0)
-
     scaled = pl.pallas_call(
         final_kernel,
-        grid_spec=pltpu.PrefetchScalarGridSpec(
-            num_scalar_prefetch=3,
-            grid=(slots // group,),
-            in_specs=[
-                pl.BlockSpec((group, size, size), in_map),
-                whole(row_scale.shape),
-                whole(col_scale.shape),
-            ],
-            out_specs=pl.BlockSpec((group, size, size), lambda g, *_: (g, 0, 0)),
-        ),
+        in_specs=[smem, smem, smem, pl.BlockSpec(memory_space=pl.ANY), vmem, vmem],
+        out_specs=pl.BlockSpec(memory_space=pl.ANY),
         out_shape=jax.ShapeDtypeStruct(values.shape, f32),
+        scratch_shapes=[
+            pltpu.VMEM(values.shape, f32),
+            pltpu.VMEM(values.shape, f32),
+            pltpu.VMEM((size, size), f32),
+            dma((slots,)),
+            dma((slots,)),
+        ],
+        compiler_params=pltpu.CompilerParams(vmem_limit_bytes=60 * 2**20),
         name="scale_tiles",
     )(rows, cols, count, values, row_scale, col_scale)
     return (row_scale.reshape(-1), col_scale.reshape(-1), scaled[None, None])

time: 97.6 us -> 92.3 us (0.946); the launches traced: 96.2 us -> 93.1 us
  Pallas kernels: 93.5 us -> 90.3 us
    pallas_call x1, Pallas kernels: 12.4 us -> 10.8 us  [shards(): pl.pallas_call(final_kernel, in_specs=[smem, smem, smem, pl.BlockSpec(mem...]
    pallas_call x1, Pallas kernels: 81.1 us -> 79.5 us  [shards(): pl.pallas_call(scale_kernel, out_shape=(jax.ShapeDtypeStruct((depths, rh,...]
where the time goes in v1:
time: 92.3 us; the launch traced here: 93.1 us
  Pallas kernels  90.3 us (98%)
  local copies, waits for them, and re-layouts  1.46 us (2%)
  between operations  1.32 us (1%)
    pallas_call x1, Pallas kernels, shards(): pl.pallas_call(scale_kernel, out_shape=(jax.ShapeDtypeStruct((depths, rh,...  79.5 us
    pallas_call x1, Pallas kernels, shards(): pl.pallas_call(final_kernel, in_specs=[smem, smem, smem, pl.BlockSpec(mem...  10.8 us

profile of v1, /device:TPU:0, one launch (start us, length us, event | category | flops | bytes accessed | tf_op | source)
XLA Modules:
  0.0 93.1 jit_solution(7058135837046387969)
XLA Ops:
  1.3 79.5 %equilibrate.1 = (f32[2,64,256]{2,1,0:T(8,128)}, f32[2,64,256]{2,1,0:T(8,128)}) custom-call(s32[48]{0:T(128)} %bitcast.22, s32[48]{0:T(128)} %bitcast.24, s32[1]{0:T(128)} %bitcast.11.count, f32[48,256,256]{2,1,0:T(8,128)} %bitcast.13), custom_call_target="tpu_custom_call" | custom-call | tf_op jit(solution)/shard_map/equilibrate/pallas_call | solution.py:266
  80.8 0.0 copy-start.1
  80.8 0.0 copy-start
  80.8 10.8 %scale_tiles.1 = f32[48,256,256]{2,1,0:T(8,128)} custom-call(s32[48]{0:T(128)} %bitcast.23, s32[48]{0:T(128)} %bitcast.25, s32[1]{0:T(128)} %bitcast.12.count, f32[48,256,256]{2,1,0:T(8,128)} %bitcast.14, f32[128,256]{1,0:T(8,128)} %bitcast.16, f32[128,256]{1,0:T(8,128)} %bitcast.18), custom_call_target="tpu_custom_call" | custom-call | tf_op jit(solution)/shard_map/scale_tiles/pallas_call | solution.py:303
  91.7 0.0 copy-done.1
  91.7 0.7 copy.8
  92.4 0.0 copy-done
  92.4 0.7 copy.7
Async XLA Ops:
  80.8 10.8 %copy-start.1 = (f32[2,64,256]{2,1,0:T(8,128)S(1)}, f32[2,64,256]{2,1,0:T(8,128)}, u32[]{:S(2)}) copy-start(f32[2,64,256]{2,1,0:T(8,128)} %get-tuple-element.6) | copy-start | bytes 393220
  80.8 11.6 %copy-start = (f32[2,64,256]{2,1,0:T(8,128)S(1)}, f32[2,64,256]{2,1,0:T(8,128)}, u32[]{:S(2)}) copy-start(f32[2,64,256]{2,1,0:T(8,128)} %get-tuple-element.5) | copy-start | bytes 393220

commit v2 on v1

--- a/solution.py
+++ b/solution.py
@@ -11,7 +11,7 @@
 ANCHORS = 16
 SWEEPS = 4
 EPS = 1e-06
-UNROLL = 8
+UNROLL = 16
 GROUP = 4
 MESH = pl.DeviceIdType.MESH
 ROUNDS = SWEEPS + 1
@@ -123,7 +123,7 @@
                 term = jnp.where(block == ids[s], part[s], jnp.float32(0.0))
                 return acc + term if summed else jnp.maximum(acc, term)
 
-            side.acc[t, d] = lax.fori_loop(0, slots, add, jnp.zeros(shape, jnp.float32), unroll=4)
+            side.acc[t, d] = lax.fori_loop(0, slots, add, jnp.zeros(shape, jnp.float32), unroll=8)
 
     def factor(side, t, index):
         return side.fac[t, index // side.hb, pl.ds(index % side.hb, 1), :]
@@ -169,7 +169,7 @@
     col.pair_to_group(0, jnp.maximum)
     row.pair_to_group(0, jnp.maximum)
 
-    @pl.loop(0, slots, unroll=4)
+    @pl.loop(0, slots, unroll=8)
     def _(s):
         mag_t[s] = mag[s].T
 

time: 92.3 us -> 90.5 us (0.980)
  the two profiles are of different devices: /device:TPU:0 before, /device:TPU:1 now
where the time goes in v2:
time: 90.5 us; the launch traced here: 90.6 us
  Pallas kernels  87.8 us (97%)
  local copies, waits for them, and re-layouts  1.46 us (2%)
  between operations  1.32 us (1%)
    pallas_call x1, Pallas kernels, shards(): pl.pallas_call(scale_kernel, out_shape=(jax.ShapeDtypeStruct((depths, rh,...  76.5 us
    pallas_call x1, Pallas kernels, shards(): pl.pallas_call(final_kernel, in_specs=[smem, smem, smem, pl.BlockSpec(mem...  11.3 us

profile of v2, /device:TPU:1, one launch (start us, length us, event | category | flops | bytes accessed | tf_op | source)
XLA Modules:
  0.0 90.6 jit_solution(12957456694414945340)
XLA Ops:
  1.3 76.5 %equilibrate.1 = (f32[2,64,256]{2,1,0:T(8,128)}, f32[2,64,256]{2,1,0:T(8,128)}) custom-call(s32[48]{0:T(128)} %bitcast.22, s32[48]{0:T(128)} %bitcast.24, s32[1]{0:T(128)} %bitcast.11.count, f32[48,256,256]{2,1,0:T(8,128)} %bitcast.13), custom_call_target="tpu_custom_call" | custom-call | tf_op jit(solution)/shard_map/equilibrate/pallas_call | solution.py:266
  77.8 0.0 copy-start.1
  77.8 0.0 copy-start
  77.8 11.3 %scale_tiles.1 = f32[48,256,256]{2,1,0:T(8,128)} custom-call(s32[48]{0:T(128)} %bitcast.23, s32[48]{0:T(128)} %bitcast.25, s32[1]{0:T(128)} %bitcast.12.count, f32[48,256,256]{2,1,0:T(8,128)} %bitcast.14, f32[128,256]{1,0:T(8,128)} %bitcast.16, f32[128,256]{1,0:T(8,128)} %bitcast.18), custom_call_target="tpu_custom_call" | custom-call | tf_op jit(solution)/shard_map/scale_tiles/pallas_call | solution.py:303
  89.1 0.0 copy-done.1
  89.1 0.7 copy.8
  89.9 0.0 copy-done
  89.9 0.7 copy.7
Async XLA Ops:
  77.8 11.3 %copy-start.1 = (f32[2,64,256]{2,1,0:T(8,128)S(1)}, f32[2,64,256]{2,1,0:T(8,128)}, u32[]{:S(2)}) copy-start(f32[2,64,256]{2,1,0:T(8,128)} %get-tuple-element.6) | copy-start | bytes 393220
  77.8 12.0 %copy-start = (f32[2,64,256]{2,1,0:T(8,128)S(1)}, f32[2,64,256]{2,1,0:T(8,128)}, u32[]{:S(2)}) copy-start(f32[2,64,256]{2,1,0:T(8,128)} %get-tuple-element.5) | copy-start | bytes 393220
